TPU v7x, 32 devices: a whole 2x2x4 slice. The times are simulated.
32 devices in a mesh: req: 16 (over z, y, x), tp: 2 (over core).
Axes of the slice: x: 2, y: 2, z: 4, core: 2. Of those that a mesh axis runs over, the one named last changes fastest.
Arguments:
- tokens: bfloat16 [2048, 2560], P('req'), may hold values from -6 to 6
- input_norm_gain: bfloat16 [2560], replicated, may hold values from 0.5 to 1.5
- query_weight: bfloat16 [2560, 4096], P(None, 'tp'), may hold values from -0.125 to 0.125
- key_value_weight: bfloat16 [2, 2560, 1024], P(None, None, 'tp'), may hold values from -0.125 to 0.125
- query_head_gain: bfloat16 [128], replicated, may hold values from 0.25 to 1.75
- key_head_gain: bfloat16 [128], replicated, may hold values from 0.25 to 1.75
- adapter_down_maps: bfloat16 [16, 48, 2560], P('req', None, 'tp'), may hold values from -0.125 to 0.125
- query_up_maps: bfloat16 [16, 16, 4096], P('req', None, 'tp'), may hold values from -0.75 to 0.75
- key_value_up_maps: bfloat16 [16, 2, 16, 1024], P('req', None, None, 'tp'), may hold values from -0.75 to 0.75
- packed_lengths: int32 [4], replicated, may hold values from 64 to 1024, as said below
- adapter_per_prompt: int32 [4], replicated, may hold values from 0 to 15, as said below
- adapter_place: int32 [16], replicated, may hold values from 0 to 15, each once
Outputs:
- attended: bfloat16 [2048, 4096], P('req', 'tp')
Inputs may be any that keep to these rules, and one draw needn't show every extreme that they name: `packed_lengths`: every entry is a multiple of 64; exactly one is 1024, at least one is 64, and they sum to 2048. `adapter_per_prompt`: the prompts use distinct adapters.
All inputs are finite; a program needn't handle non-finite values.
Results may differ from a plain program's by a relative error of at most 0.0086.
Values may be sent and summed in bfloat16 or wider, within the bound.
A program may use at most 128 MiB of HBM per device.

v0:
```python
import math
import jax
import jax.numpy as jnp
from jax import lax
from jax.sharding import PartitionSpec as P

SHORT_LEN = 64
epsilon = 1e-06
theta = 1000000.0
adapter_scale = 2.0


def normalize(values, gain_vec):
    values = values.astype(jnp.float32)
    inverse = lax.rsqrt(jnp.mean(values * values, axis=-1, keepdims=True) + epsilon)
    return values * inverse * gain_vec.astype(jnp.float32)


def rotate(values, offsets):
    half_dim = values.shape[-1] // 2
    powers = jnp.arange(half_dim, dtype=jnp.float32) * (2.0 / values.shape[-1])
    frequency = theta ** (-powers)
    angles = offsets.astype(jnp.float32)[:, None] * frequency[None, :]
    cosine = jnp.cos(angles)[:, None, :]
    sine_part = jnp.sin(angles)[:, None, :]
    former = values[..., :half_dim]
    latter = values[..., half_dim:]
    return jnp.concatenate(
        [former * cosine - latter * sine_part, latter * cosine + former * sine_part], axis=-1
    )


def doc_start(positions, packed_lengths):
    doc_end = jnp.cumsum(packed_lengths)
    return jnp.sum(
        jnp.where(doc_end[None, :] <= positions[:, None], packed_lengths[None, :], 0), axis=1
    )


def holders(positions, packed_lengths, adapter_per_prompt, adapter_place):
    doc_end = jnp.cumsum(packed_lengths)
    inside = (doc_end[None, :] > positions[:, None]) & (
        doc_end[None, :] - packed_lengths[None, :] <= positions[:, None]
    )
    adapter = jnp.sum(jnp.where(inside, adapter_per_prompt[None, :], 0), axis=1)
    catalog = jnp.arange(adapter_place.shape[0], dtype=jnp.int32)
    return jnp.sum(
        jnp.where(adapter[:, None] == catalog[None, :], adapter_place[None, :], 0), axis=1
    )


def on_device(
    tokens,
    input_norm_gain,
    query_weight,
    key_value_weight,
    query_head_gain,
    key_head_gain,
    adapter_down_maps,
    query_up_maps,
    key_value_up_maps,
    packed_lengths,
    adapter_per_prompt,
    adapter_place,
):
    token_rows = tokens.shape[0]
    first_row = lax.axis_index("req") * token_rows
    positions = first_row + jnp.arange(token_rows, dtype=jnp.int32)
    starts = doc_start(positions, packed_lengths)
    owners = holders(positions, packed_lengths, adapter_per_prompt, adapter_place)
    unit_count = token_rows // SHORT_LEN
    unit_owner = owners[::SHORT_LEN]
    normed = normalize(tokens, input_norm_gain).astype(jnp.bfloat16)
    plain_query = jnp.dot(normed, query_weight, preferred_element_type=jnp.float32)
    plain_pair = jnp.einsum(
        "td,cdk->ctk", normed, key_value_weight, preferred_element_type=jnp.float32
    )
    rank_width = query_up_maps.shape[1]
    local_width = adapter_down_maps.shape[2]
    own_cols = lax.dynamic_slice_in_dim(normed, lax.axis_index("tp") * local_width, local_width, 1)
    pieces = (
        lax.all_gather(adapter_down_maps, "req", axis=0, tiled=True),
        lax.all_gather(query_up_maps, "req", axis=0, tiled=True),
        lax.all_gather(key_value_up_maps, "req", axis=0, tiled=True),
    )
    piece_count = pieces[0].shape[0]
    slots_here = jnp.arange(piece_count, dtype=jnp.int32)
    chosen = (unit_owner[:, None] == slots_here[None, :]).astype(jnp.bfloat16)
    down_sel = jnp.einsum(
        "uk,krd->urd", chosen, pieces[0], preferred_element_type=jnp.float32
    ).astype(jnp.bfloat16)
    upq_sel = jnp.einsum(
        "uk,krc->urc", chosen, pieces[1], preferred_element_type=jnp.float32
    ).astype(jnp.bfloat16)
    upkv_sel = jnp.einsum(
        "uk,kcrd->ucrd", chosen, pieces[2], preferred_element_type=jnp.float32
    ).astype(jnp.bfloat16)
    partial_sum = jnp.einsum(
        "utd,urd->utr",
        own_cols.reshape(unit_count, SHORT_LEN, local_width),
        down_sel,
        preferred_element_type=jnp.float32,
    )
    reduced_rank = lax.psum(partial_sum, "tp").astype(jnp.bfloat16)
    query_increment = jnp.einsum(
        "utr,urc->utc", reduced_rank[..., :rank_width], upq_sel, preferred_element_type=jnp.float32
    ).reshape(token_rows, -1)
    pair_rank = reduced_rank[..., rank_width:].reshape(unit_count, SHORT_LEN, 2, rank_width)
    pair_increment = jnp.einsum(
        "utcr,ucrk->cutk", pair_rank, upkv_sel, preferred_element_type=jnp.float32
    ).reshape(2, token_rows, -1)
    head_width = query_head_gain.shape[0]
    query_heads = query_weight.shape[1] // head_width
    key_value_heads = key_value_weight.shape[2] // head_width
    group_width = query_heads // key_value_heads
    offsets = positions - starts
    query_rotated = (plain_query + adapter_scale * query_increment).reshape(
        token_rows, query_heads, head_width
    )
    query_rotated = rotate(normalize(query_rotated, query_head_gain), offsets).astype(jnp.bfloat16)
    query_every_token = query_rotated.reshape(token_rows, key_value_heads, group_width, head_width)
    key_rotated = (plain_pair[0] + adapter_scale * pair_increment[0]).reshape(
        token_rows, key_value_heads, head_width
    )
    key_rotated = rotate(normalize(key_rotated, key_head_gain), offsets).astype(jnp.bfloat16)
    value_every_token = (
        (plain_pair[1] + adapter_scale * pair_increment[1])
        .reshape(token_rows, key_value_heads, head_width)
        .astype(jnp.bfloat16)
    )
    key_value = jnp.stack([key_rotated, value_every_token], axis=1)
    start_sums = (
        jnp.zeros((token_rows, key_value_heads, group_width), jnp.float32),
        jnp.zeros((token_rows, key_value_heads, group_width, head_width), jnp.float32),
    )
    segment = lax.all_gather(key_value, "req", axis=0, tiled=True)
    length_now = segment.shape[0]
    key_rows = max(
        (size_try for size_try in range(1, min(length_now, 1024) + 1) if length_now % size_try == 0)
    )
    block_count = length_now // key_rows
    blocks = segment.reshape(block_count, key_rows, 2, key_value_heads, head_width)
    block_first = jnp.int32(0) + key_rows * jnp.arange(block_count, dtype=jnp.int32)

    def key_step(running, block_entry):
        key_block, block_start = block_entry
        key_pos = block_start + jnp.arange(key_rows, dtype=jnp.int32)
        key_start = doc_start(key_pos, packed_lengths)
        visible = (
            (key_start[None, :] == starts[:, None])
            & (key_pos[None, :] <= positions[:, None])
            & (key_pos[None, :] >= 0)
        )
        scores = jnp.einsum(
            "tkgd,skd->tkgs", query_every_token, key_block[:, 0], preferred_element_type=jnp.float32
        ) / math.sqrt(head_width)
        weights = jnp.where(visible[:, None, None, :], jnp.exp(scores), 0.0)
        totals = running[0] + jnp.sum(weights, axis=-1)
        numerator = running[1] + jnp.einsum(
            "tkgs,skd->tkgd",
            weights.astype(jnp.bfloat16),
            key_block[:, 1],
            preferred_element_type=jnp.float32,
        )
        return ((totals, numerator), None)

    result = lax.scan(key_step, start_sums, (blocks, block_first))[0]
    output_rows = result[1] / result[0][..., None]
    return output_rows.reshape(token_rows, query_heads * head_width).astype(jnp.bfloat16)


def solution(mesh):
    in_specs = (
        P("req", None),
        P(),
        P(None, "tp"),
        P(None, None, "tp"),
        P(),
        P(),
        P("req", None, "tp"),
        P("req", None, "tp"),
        P("req", None, None, "tp"),
        P(),
        P(),
        P(),
    )
    out_specs = P("req", "tp")
    return jax.shard_map(
        on_device, mesh=mesh, in_specs=in_specs, out_specs=out_specs, check_vma=False
    )
```

profile of v0, /device:TPU:0, one launch (start us, length us, event | category | flops | bytes accessed | tf_op | source)
XLA Modules:
  0.0 245.9 jit_solution(10807951525644673926)
XLA Ops:
  6.5 0.7 all-gather.4.cloned.1.call-update
  7.3 0.7 all-gather.8.cloned.1.call-update
  8.1 0.8 reduce-window.9
  8.9 0.7 bitcast_subtract_fusion
  9.6 46.1 %all_gather.13 = bf16[16,2,16,512]{3,2,1,0:T(8,128)(2,1)S(1)} all-gather(bf16[1,2,16,512]{3,2,1,0:T(8,128)(2,1)} %param.22), channel_id=1, replica_groups=mesh['req'=16,'tp'=2] {'req'}, dimensions={0}, use_global_device_ids=true | all-gather | bytes 557056 | tf_op jit(solution)/shard_map/all_gather | solution.py:84
  55.7 0.8 select_reduce_fusion.2
  56.4 0.8 select_reduce_fusion.1
  57.3 0.7 convert_element_type.67
  58.0 1.3 fusion.20
  59.3 1.3 fusion.22
  60.6 3.4 %convolution_bitcast_fusion = f32[2,128,512]{2,1,0:T(8,128)S(1)} fusion(bf16[2,2560,512]{2,1,0:T(8,128)(2,1)} %param.17, bf16[128,2560]{1,0:T(8,128)(2,1)S(1)} %fusion.22), kind=kOutput, calls=%fused_computation.33 | convolution fusion | flops 671088640 | bytes 6422528 | tf_op jit(solution)/shard_map/td,cdk->ctk/dot_general | solution.py:75
  64.3 0.4 convolution_convert_fusion.2
  64.7 0.3 multiply_cosine_fusion
  65.0 8.9 %all-gather.4.cloned.1.call-done = bf16[16,48,1280]{2,1,0:T(8,128)(2,1)} async-done(((bf16[1,48,1280]{2,1,0:T(8,128)(2,1)}), bf16[16,48,1280]{2,1,0:T(8,128)(2,1)}) %all-gather.4.cloned.1.call-update) | async-done | bytes 1966096 | tf_op jit(solution)/shard_map/all_gather | solution.py:82
  74.0 2.3 convolution_convert_fusion
  76.2 0.2 fusion.27
  76.4 3.7 %psum.7 = bf16[2,64,48]{1,2,0:T(8,128)(2,1)S(1)} all-reduce(f32[2,64,48]{1,2,0:T(8,128)S(1)} %fusion.27), channel_id=1, replica_groups=mesh['req'=16,'tp'=2] {'tp'}, use_global_device_ids=true, to_apply=%region_4.5 | all-reduce | flops 6144 | bytes 36864 | tf_op jit(solution)/shard_map/psum | solution.py:104
  80.2 0.3 fusion.32
  80.7 0.1 multiply_reduce_fusion.1
  81.0 0.1 fusion.29
  81.2 0.8 pad_maximum_fusion.1
  82.0 0.2 broadcast_in_dim.65
  82.2 48.5 %all-gather.8.cloned.1.call-done = bf16[16,16,2048]{2,1,0:T(8,128)(2,1)} async-done(((bf16[1,16,2048]{2,1,0:T(8,128)(2,1)}), bf16[16,16,2048]{2,1,0:T(8,128)(2,1)}) %all-gather.8.cloned.1.call-update) | async-done | bytes 1048592 | tf_op jit(solution)/shard_map/all_gather | solution.py:83
  130.7 2.4 convolution_convert_fusion.1
  133.1 0.3 convolution_multiply_fusion
  133.5 5.5 %fusion.19 = f32[16,8,16,128]{3,1,2,0:T(8,128)S(1)} fusion(f32[128,2048]{1,0:T(8,128)S(1)} %bitcast.99, bf16[128,2560]{1,0:T(8,128)(2,1)S(1)} %fusion.22, bf16[2560,2048]{1,0:T(8,128)(2,1)} %param.16), kind=kOutput, calls=%fused_computation.29 | convolution fusion | flops 1342439424 | bytes 13238272 | tf_op jit(solution)/shard_map/dot_general | solution.py:74
  139.0 0.2 copy.109
  139.2 0.3 multiply_reduce_fusion
  139.7 0.3 multiply_multiply_fusion
  140.1 0.5 subtract_convert_fusion
  140.9 1.1 pad_maximum_fusion
  142.0 66.8 %all-gather.6.cloned.1.call-done = bf16[2048,2,4,128]{3,0,2,1:T(8,128)(2,1)} async-done(((bf16[128,2,4,128]{3,0,2,1:T(8,128)(2,1)}), bf16[2048,2,4,128]{3,0,2,1:T(8,128)(2,1)}) %all-gather.6.cloned.1.call-update) | async-done | bytes 4194320 | tf_op jit(solution)/shard_map/all_gather | solution.py:136
  208.8 29.5 %while.14 = (s32[]{:T(128)}, f32[128,4,4]{0,2,1:T(4,128)S(1)}, f32[128,4,4,128]{0,3,2,1:T(8,128)S(1)}, s32[1,4]{1,0:T(1,128)S(1)}, s32[2]{0:T(128)S(1)}, /*index...) while((s32[]{:T(128)}, f32[128,4,4]{0,2,1:T(4,128)S(1)}, ...), condition=%wide.region_12.13_spmd.clone, body=%wide.region_9.12_spmd.clone.sunk | while | flops 1087389824 | bytes 28237536 | solution.py:167
  208.8 0.7 dynamic_slice.21
  209.4 0.7 iota_add_fusion.6
  210.2 0.7 broadcast_compare_fusion.2
  210.9 0.9 and_and_fusion.2
  211.8 1.7 dynamic-slice_bitcast_fusion.2
  213.6 4.9 %fusion.54 = (f32[128,4,4]{0,2,1:T(4,128)S(1)}, f32[4,1024,128,4]{2,1,3,0:T(8,128)}) fusion(pred[128,1024]{0,1:T(8,128)(4,1)S(1)} %and_and_fusion.2, bf16[128,4,4,128]{3,0,2,1:T(8,128)(2,1)S(1)} %copy-done, bf16[1024,2,4,128]{3,0,2,1:T(8,128)(2,1)S(1)} %dynamic-slice_bitcast_fusion.2), kind=kOutput, calls=%fused_computation.3.clone.1 | convolution fusion | flops 543160320 | bytes 10100736 | tf_op jit(solution)/shard_map/while/body/eval_jaxpr/tkgd,skd->tkgs/dot_general | solution.py:154
  218.5 4.9 %fusion.55 = f32[128,4,4,128]{0,3,2,1:T(8,128)S(1)} fusion(f32[4,1024,128,4]{2,1,3,0:T(8,128)} %get-tuple-element.280, pred[128,1024]{0,1:T(8,128)(4,1)S(1)} %and_and_fusion.2, bf16[1024,2,4,128]{3,0,2,1:T(8,128)(2,1)S(1)} %dynamic-slice_bitcast_fusion.2, f32[128,4,4,128]{0,3,2,1:T(8,128)S(1)} %get-tuple-element.295, pred[]{:T(512)S(6)} %compare.3), kind=kOutput, calls=%fused_computation.10.clone.1 | convolution fusion | flops 543686656 | bytes 11665409 | tf_op jit(solution)/shard_map/while/body/eval_jaxpr/tkgs,skd->tkgd/dot_general | solution.py:159
  223.5 0.7 dynamic_slice.21
  224.2 0.7 iota_add_fusion.6
  225.0 0.7 broadcast_compare_fusion.2
  225.7 0.9 and_and_fusion.2
  226.6 1.7 dynamic-slice_bitcast_fusion.2
  228.3 4.9 %fusion.54 = (f32[128,4,4]{0,2,1:T(4,128)S(1)}, f32[4,1024,128,4]{2,1,3,0:T(8,128)}) fusion(pred[128,1024]{0,1:T(8,128)(4,1)S(1)} %and_and_fusion.2, bf16[128,4,4,128]{3,0,2,1:T(8,128)(2,1)S(1)} %copy-done, bf16[1024,2,4,128]{3,0,2,1:T(8,128)(2,1)S(1)} %dynamic-slice_bitcast_fusion.2), kind=kOutput, calls=%fused_computation.3.clone.1 | convolution fusion | flops 543160320 | bytes 10100736 | tf_op jit(solution)/shard_map/while/body/eval_jaxpr/tkgd,skd->tkgs/dot_general | solution.py:154
  233.3 4.9 %fusion.55 = f32[128,4,4,128]{0,3,2,1:T(8,128)S(1)} fusion(f32[4,1024,128,4]{2,1,3,0:T(8,128)} %get-tuple-element.280, pred[128,1024]{0,1:T(8,128)(4,1)S(1)} %and_and_fusion.2, bf16[1024,2,4,128]{3,0,2,1:T(8,128)(2,1)S(1)} %dynamic-slice_bitcast_fusion.2, f32[128,4,4,128]{0,3,2,1:T(8,128)S(1)} %get-tuple-element.295, pred[]{:T(512)S(6)} %compare.3), kind=kOutput, calls=%fused_computation.10.clone.1 | convolution fusion | flops 543686656 | bytes 11665409 | tf_op jit(solution)/shard_map/while/body/eval_jaxpr/tkgs,skd->tkgd/dot_general | solution.py:159
  238.4 1.0 copy.105
  (47 shorter events, 1.7 us)
Async XLA Ops:
  6.5 67.4 %all-gather.4.cloned.1.call-start = ((), (), s32[]{:S(2)}) async-start(), calls=%async_computation | async-start | bytes 2088960 | tf_op jit(solution)/shard_map/all_gather | solution.py:82
  7.3 123.4 %all-gather.8.cloned.1.call-start = ((), (), s32[]{:S(2)}) async-start(), calls=%async_computation.2 | async-start | bytes 1114112 | tf_op jit(solution)/shard_map/all_gather | solution.py:83
  8.0 200.8 %all-gather.6.cloned.1.call-start = ((), (), s32[]{:S(2)}) async-start(), calls=%async_computation.1 | async-start | bytes 4456448 | tf_op jit(solution)/shard_map/all_gather | solution.py:136
  60.6 3.5 %copy-start.2 = (bf16[128]{0:T(256)(128)(2,1)S(1)}, bf16[128]{0:T(256)(128)(2,1)}, u32[]{:S(2)}) copy-start(bf16[128]{0:T(256)(128)(2,1)} %param.19) | copy-start | bytes 772
  65.0 17.0 %copy-start.1 = (s32[4]{0:T(128)S(1)}, s32[4]{0:T(128)}, u32[]{:S(2)}) copy-start(s32[4]{0:T(128)} %param.23) | copy-start | bytes 52
  65.0 17.2 %copy-start.3 = (bf16[128]{0:T(256)(128)(2,1)S(1)}, bf16[128]{0:T(256)(128)(2,1)}, u32[]{:S(2)}) copy-start(bf16[128]{0:T(256)(128)(2,1)} %param.18) | copy-start | bytes 772
  208.8 4.8 %copy-start = (bf16[128,4,4,128]{3,0,2,1:T(8,128)(2,1)S(1)}, bf16[128,4,4,128]{3,0,2,1:T(8,128)(2,1)}, u32[]{:S(2)}) copy-start(bf16[128,4,4,128]{3,0,2,1:T(8,128)(2,1)} %get-tuple-element.313) | copy-start | bytes 1572868 | tf_op jit(solution)/shard_map/while
  223.5 4.8 %copy-start = (bf16[128,4,4,128]{3,0,2,1:T(8,128)(2,1)S(1)}, bf16[128,4,4,128]{3,0,2,1:T(8,128)(2,1)}, u32[]{:S(2)}) copy-start(bf16[128,4,4,128]{3,0,2,1:T(8,128)(2,1)} %get-tuple-element.313) | copy-start | bytes 1572868 | tf_op jit(solution)/shard_map/while
Sparse Core Ops, SparseCore 0:
  10.2 63.7 all-gather.3
  76.7 53.9 all-gather.7
  133.4 75.2 all-gather.5
where the time goes:
time: 247 us; the launch traced here: 246 us
  waiting for transfers between devices  126 us (51%)
  blocking collectives  49.8 us (20%)
  matrix products  34.5 us (14%)
  other arithmetic  15.3 us (6%)
  between operations  13.4 us (5%)
  local copies, waits for them, and re-layouts  7.03 us (3%)
    all_gather x1, waiting for transfers between devices, on_device(): segment = lax.all_gather(key_value, 'req', axis=0, tiled=True)  66.8 us
    all_gather x1, waiting for transfers between devices, on_device(): lax.all_gather(query_up_maps, 'req', axis=0, tiled=True)  48.5 us
    all_gather x1, blocking collectives, on_device(): lax.all_gather(key_value_up_maps, 'req', axis=0, tiled=True)  46.1 us
    dot_general x2, matrix products, key_step(): jnp.einsum('tkgs,skd->tkgd', weights.astype(jnp.bfloat16), key_block[:, 1...  9.88 us
    dot_general x2, matrix products, key_step(): jnp.einsum('tkgd,skd->tkgs', query_every_token, key_block[:, 0], preferre...  9.85 us
    all_gather x1, waiting for transfers between devices, on_device(): lax.all_gather(adapter_down_maps, 'req', axis=0, tiled=True)  8.92 us
    dot_general x1, matrix products, on_device(): jnp.dot(normed, query_weight, preferred_element_type=jnp.float32)  5.51 us
  transfers between devices with their start and end apart: 3, of which 3 were waited for; matrix products, arithmetic and copies ran while one was open for 11% of the time, Pallas kernels for 0%

commit v1 on v0

--- a/solution.py
+++ b/solution.py
@@ -8,6 +8,28 @@
 epsilon = 1e-06
 theta = 1000000.0
 adapter_scale = 2.0
+
+
+def joined_along(blocks, dim):
+    shape = list(blocks.shape[1:])
+    shape[dim] *= blocks.shape[0]
+    return jnp.moveaxis(blocks, 0, dim).reshape(shape)
+
+
+def ring_gather(x, axis, dim):
+    size = lax.axis_size(axis)
+    pairs = [(i, (i + 1) % size) for i in range(size)]
+    back = [(b, a) for a, b in pairs]
+    lower, upper = ([], [])
+    for step in range(size - 1):
+        if step % 2 == 0:
+            lower.append(lax.ppermute(lower[-1] if lower else x, axis, pairs))
+        else:
+            upper.append(lax.ppermute(upper[-1] if upper else x, axis, back))
+    blocks = jnp.stack([*lower[::-1], x, *upper])
+    shift = lax.axis_index(axis) - len(lower)
+    blocks = blocks[(jnp.arange(size) - shift) % size]
+    return joined_along(blocks, dim)
 
 
 def normalize(values, gain_vec):
@@ -80,7 +102,7 @@
     own_cols = lax.dynamic_slice_in_dim(normed, lax.axis_index("tp") * local_width, local_width, 1)
     pieces = (
         lax.all_gather(adapter_down_maps, "req", axis=0, tiled=True),
-        lax.all_gather(query_up_maps, "req", axis=0, tiled=True),
+        ring_gather(query_up_maps, "req", 0),
         lax.all_gather(key_value_up_maps, "req", axis=0, tiled=True),
     )
     piece_count = pieces[0].shape[0]

time: 247 us -> 246 us (level)
  waiting for transfers between devices: 126 us -> 73.8 us
  starting transfers between devices: 0.08 us -> 42.2 us
  local copies, waits for them, and re-layouts: 7.03 us -> 14.5 us
  other arithmetic: 15.3 us -> 18.9 us
  blocking collectives: 49.8 us -> 46.3 us
    all_gather x1 -> x0, waiting for transfers between devices: 48.5 us -> none  [on_device(): lax.all_gather(query_up_maps, 'req', axis=0, tiled=True)]
    ppermute x0 -> x15, starting transfers between devices: none -> 42.1 us  [the longest x7 39.1 us: ring_gather(): upper.append(lax.ppermute(upper[-1] if upper else x, axis, back))]
    ppermute x0 -> x15, waiting for transfers between devices: none -> 18 us  [the longest x8 13 us: ring_gather(): lower.append(lax.ppermute(lower[-1] if lower else x, axis, pairs))]
    all_gather x1, waiting for transfers between devices: 66.8 us -> 55.8 us  [on_device(): segment = lax.all_gather(key_value, 'req', axis=0, tiled=True)]
    all_gather x1, waiting for transfers between devices: 8.92 us -> 0.02 us  [on_device(): lax.all_gather(adapter_down_maps, 'req', axis=0, tiled=True)]
    unnamed x7 -> x64, local copies, waits for them, and re-layouts: 0.21 us -> 6.27 us
    all_gather x1, blocking collectives: 46.1 us -> 42.4 us  [on_device(): lax.all_gather(key_value_up_maps, 'req', axis=0, tiled=True)]
  transfers between devices with their start and end apart: 3 -> 17, of which waited for: 3 -> 7; matrix products, arithmetic and copies ran while one was open for 11% -> 14% of each run, Pallas kernels for 0% -> 0%
where the time goes in v1:
time: 246 us; the launch traced here: 245 us
  waiting for transfers between devices  73.8 us (30%)
  blocking collectives  46.3 us (19%)
  starting transfers between devices  42.2 us (17%)
  matrix products  35.4 us (14%)
  other arithmetic  18.9 us (8%)
  local copies, waits for them, and re-layouts  14.5 us (6%)
  between operations  14 us (6%)
    all_gather x1, waiting for transfers between devices, on_device(): segment = lax.all_gather(key_value, 'req', axis=0, tiled=True)  55.8 us
    all_gather x1, blocking collectives, on_device(): lax.all_gather(key_value_up_maps, 'req', axis=0, tiled=True)  42.4 us
    ppermute x7, starting transfers between devices, ring_gather(): upper.append(lax.ppermute(upper[-1] if upper else x, axis, back))  39.1 us
    ppermute x8, waiting for transfers between devices, ring_gather(): lower.append(lax.ppermute(lower[-1] if lower else x, axis, pairs))  13 us
    dot_general x2, matrix products, key_step(): jnp.einsum('tkgs,skd->tkgd', weights.astype(jnp.bfloat16), key_block[:, 1...  11.8 us
    dot_general x2, matrix products, key_step(): jnp.einsum('tkgd,skd->tkgs', query_every_token, key_block[:, 0], preferre...  9.86 us
    unnamed x64, local copies, waits for them, and re-layouts  6.27 us
    dot_general x1, matrix products, on_device(): jnp.dot(normed, query_weight, preferred_element_type=jnp.float32)  5.54 us
  transfers between devices with their start and end apart: 17, of which 7 were waited for; matrix products, arithmetic and copies ran while one was open for 14% of the time, Pallas kernels for 0%

profile of v1, /device:TPU:0, one launch (start us, length us, event | category | flops | bytes accessed | tf_op | source)
XLA Modules:
  0.0 245.2 jit_solution(3321009628766194033)
XLA Ops:
  6.5 2.9 %collective-permute-start = (bf16[1,16,2048]{2,1,0:T(8,128)(2,1)}, bf16[1,16,2048]{2,1,0:T(8,128)(2,1)S(1)}, u32[]{:S(2)}, u32[]{:S(2)}) collective-permute-start(bf16[1,16,2048]{2,1,0:T(8,128)(2,1)} %param.21), channel_id=1, source_target_pairs={{0,2},{2,4},{4,6},{6,8},{8,10},{10,12},{12,14},{14,16},{16,18},{18... | collective-permute-start | bytes 196616 | tf_op jit(solution)/shard_map/ppermute | solution.py:26
  9.5 4.0 %collective-permute-start.8 = (bf16[1,16,2048]{2,1,0:T(8,128)(2,1)}, bf16[1,16,2048]{2,1,0:T(8,128)(2,1)S(1)}, u32[]{:S(2)}, u32[]{:S(2)}) collective-permute-start(bf16[1,16,2048]{2,1,0:T(8,128)(2,1)} %param.21), channel_id=1, source_target_pairs={{2,0},{4,2},{6,4},{8,6},{10,8},{12,10},{14,12},{16,14},{18,16},{20... | collective-permute-start | bytes 196616 | tf_op jit(solution)/shard_map/ppermute | solution.py:28
  13.6 0.8 reduce-window.9
  15.7 1.3 fusion.20
  17.1 1.3 fusion.22
  18.4 0.8 select_reduce_fusion.2
  19.1 0.7 select_reduce_fusion.1
  20.0 3.5 %convolution_bitcast_fusion = f32[2,128,512]{2,1,0:T(8,128)S(1)} fusion(bf16[2,2560,512]{2,1,0:T(8,128)(2,1)} %param.17, bf16[128,2560]{1,0:T(8,128)(2,1)S(1)} %fusion.22), kind=kOutput, calls=%fused_computation.34 | convolution fusion | flops 671088640 | bytes 6422528 | tf_op jit(solution)/shard_map/td,cdk->ctk/dot_general | solution.py:97
  23.5 42.4 %all_gather.10 = bf16[16,2,16,512]{3,2,1,0:T(8,128)(2,1)S(1)} all-gather(bf16[1,2,16,512]{3,2,1,0:T(8,128)(2,1)S(1)} %copy-done.15), channel_id=1, replica_groups=mesh['req'=16,'tp'=2] {'req'}, dimensions={0}, use_global_device_ids=true | all-gather | bytes 557056 | tf_op jit(solution)/shard_map/all_gather | solution.py:106
  66.5 8.5 %collective-permute-done.1 = bf16[1,16,2048]{2,1,0:T(8,128)(2,1)S(1)} collective-permute-done((bf16[1,16,2048]{2,1,0:T(8,128)(2,1)S(1)}, bf16[1,16,2048]{2,1,0:T(8,128)(2,1)S(1)}, u32[]{:S(2)}, u32[]{:S(2)}) %collective-permute-start.1) | collective-permute-done | bytes 65568 | tf_op jit(solution)/shard_map/ppermute | solution.py:26
  75.0 5.7 %collective-permute-start.9 = (bf16[1,16,2048]{2,1,0:T(8,128)(2,1)S(1)}, bf16[1,16,2048]{2,1,0:T(8,128)(2,1)S(1)}, u32[]{:S(2)}, u32[]{:S(2)}) collective-permute-start(bf16[1,16,2048]{2,1,0:T(8,128)(2,1)S(1)} %collective-permute-done.8), channel_id=1, source_target_pairs={{2,0},{4,2},{6,4},{8,6},{10,8},{12,10},{14,12},{16,14},{18,16},{20... | collective-permute-start | bytes 196616 | tf_op jit(solution)/shard_map/ppermute | solution.py:28
  80.7 2.2 collective-permute-done.2
  83.0 5.7 %collective-permute-start.10 = (bf16[1,16,2048]{2,1,0:T(8,128)(2,1)S(1)}, bf16[1,16,2048]{2,1,0:T(8,128)(2,1)S(1)}, u32[]{:S(2)}, u32[]{:S(2)}) collective-permute-start(bf16[1,16,2048]{2,1,0:T(8,128)(2,1)S(1)} %collective-permute-done.9), channel_id=1, source_target_pairs={{2,0},{4,2},{6,4},{8,6},{10,8},{12,10},{14,12},{16,14},{18,16},{20... | collective-permute-start | bytes 196616 | tf_op jit(solution)/shard_map/ppermute | solution.py:28
  88.6 2.2 collective-permute-done.3
  91.2 0.8 broadcast_in_dim.65
  93.2 5.6 %collective-permute-start.11 = (bf16[1,16,2048]{2,1,0:T(8,128)(2,1)S(1)}, bf16[1,16,2048]{2,1,0:T(8,128)(2,1)S(1)}, u32[]{:S(2)}, u32[]{:S(2)}) collective-permute-start(bf16[1,16,2048]{2,1,0:T(8,128)(2,1)S(1)} %collective-permute-done.10), channel_id=1, source_target_pairs={{2,0},{4,2},{6,4},{8,6},{10,8},{12,10},{14,12},{16,14},{18,16},{20... | collective-permute-start | bytes 196616 | tf_op jit(solution)/shard_map/ppermute | solution.py:28
  98.9 2.4 collective-permute-done.11
  101.2 6.1 %collective-permute-start.12 = (bf16[1,16,2048]{2,1,0:T(8,128)(2,1)S(1)}, bf16[1,16,2048]{2,1,0:T(8,128)(2,1)S(1)}, u32[]{:S(2)}, u32[]{:S(2)}) collective-permute-start(bf16[1,16,2048]{2,1,0:T(8,128)(2,1)S(1)} %collective-permute-done.11), channel_id=1, source_target_pairs={{2,0},{4,2},{6,4},{8,6},{10,8},{12,10},{14,12},{16,14},{18,16},{20... | collective-permute-start | bytes 196616 | tf_op jit(solution)/shard_map/ppermute | solution.py:28
  107.9 1.3 collective-permute-done.12
  109.2 6.0 %collective-permute-start.13 = (bf16[1,16,2048]{2,1,0:T(8,128)(2,1)S(1)}, bf16[1,16,2048]{2,1,0:T(8,128)(2,1)}, u32[]{:S(2)}, u32[]{:S(2)}) collective-permute-start(bf16[1,16,2048]{2,1,0:T(8,128)(2,1)S(1)} %collective-permute-done.12), channel_id=1, source_target_pairs={{2,0},{4,2},{6,4},{8,6},{10,8},{12,10},{14,12},{16,14},{18,16},{20... | collective-permute-start | bytes 196616 | tf_op jit(solution)/shard_map/ppermute | solution.py:28
  115.8 1.4 collective-permute-done.13
  117.1 6.1 %collective-permute-start.14 = (bf16[1,16,2048]{2,1,0:T(8,128)(2,1)}, bf16[1,16,2048]{2,1,0:T(8,128)(2,1)}, u32[]{:S(2)}, u32[]{:S(2)}) collective-permute-start(bf16[1,16,2048]{2,1,0:T(8,128)(2,1)} %collective-permute-done.13), channel_id=1, source_target_pairs={{2,0},{4,2},{6,4},{8,6},{10,8},{12,10},{14,12},{16,14},{18,16},{20... | collective-permute-start | bytes 196616 | tf_op jit(solution)/shard_map/ppermute | solution.py:28
  123.3 2.3 convolution_convert_fusion
  125.8 3.8 %psum.7 = bf16[2,64,48]{1,2,0:T(8,128)(2,1)S(1)} all-reduce(f32[2,64,48]{1,2,0:T(8,128)S(1)} %fusion.27), channel_id=1, replica_groups=mesh['req'=16,'tp'=2] {'tp'}, use_global_device_ids=true, to_apply=%region_4.5 | all-reduce | flops 6144 | bytes 36864 | tf_op jit(solution)/shard_map/psum | solution.py:126
  130.5 0.8 multiply_multiply_fusion.1
  131.4 0.8 pad_maximum_fusion.1
  132.2 0.8 bitcast_dynamic-update-slice_fusion.12
  133.1 0.8 bitcast_dynamic-update-slice_fusion.10
  133.9 0.8 bitcast_dynamic-update-slice_fusion.9
  134.8 0.8 bitcast_dynamic-update-slice_fusion.8
  135.6 0.8 bitcast_dynamic-update-slice_fusion.6
  136.6 0.8 bitcast_dynamic-update-slice_fusion.2
  137.4 0.8 bitcast_dynamic-update-slice_fusion.1
  138.3 0.8 bitcast_dynamic-update-slice_fusion
  139.9 1.2 convolution_convert_fusion.1
  141.4 5.5 %fusion.19 = f32[16,8,16,128]{3,1,2,0:T(8,128)S(1)} fusion(f32[128,2048]{1,0:T(8,128)S(1)} %bitcast.134, bf16[128,2560]{1,0:T(8,128)(2,1)S(1)} %fusion.22, bf16[2560,2048]{1,0:T(8,128)(2,1)} %param.16), kind=kOutput, calls=%fused_computation.30 | convolution fusion | flops 1342439424 | bytes 13238272 | tf_op jit(solution)/shard_map/dot_general | solution.py:96
  149.2 55.8 %all-gather.5.cloned.1.call-done = bf16[2048,2,4,128]{3,0,2,1:T(8,128)(2,1)} async-done(((bf16[128,2,4,128]{3,0,2,1:T(8,128)(2,1)}), bf16[2048,2,4,128]{3,0,2,1:T(8,128)(2,1)}) %all-gather.5.cloned.1.call-update) | async-done | bytes 4194320 | tf_op jit(solution)/shard_map/all_gather | solution.py:158
  205.0 31.0 %while.14 = (s32[]{:T(128)}, f32[128,4,4]{0,2,1:T(4,128)S(1)}, f32[128,4,4,128]{0,3,2,1:T(8,128)}, s32[1,4]{1,0:T(1,128)S(1)}, s32[2]{0:T(128)S(1)}, /*index=5*/...) while((s32[]{:T(128)}, f32[128,4,4]{0,2,1:T(4,128)S(1)}, ...), condition=%wide.region_12.13_spmd.clone, body=%wide.region_9.12_spmd.clone.sunk | while | flops 1087389824 | bytes 26140356 | solution.py:189
  207.0 0.9 and_and_fusion.2
  207.9 1.7 dynamic-slice_bitcast_fusion.2
  209.6 4.9 %fusion.56 = (f32[128,4,4]{0,2,1:T(4,128)S(1)}, f32[4,1024,128,4]{2,1,3,0:T(8,128)}) fusion(pred[128,1024]{0,1:T(8,128)(4,1)S(1)} %and_and_fusion.2, bf16[128,4,4,128]{3,0,2,1:T(8,128)(2,1)S(1)} %get-tuple-element.313, bf16[1024,2,4,128]{3,0,2,1:T(8,128)(2,1)S(1)} %dynamic-slice_bitcast_fusion.2), kind=kOutput, calls=%fused_computation.4.clone.1 | convolution fusion | flops 543160320 | bytes 10100736 | tf_op jit(solution)/shard_map/while/body/eval_jaxpr/tkgd,skd->tkgs/dot_general | solution.py:176
  214.6 5.8 %fusion.57 = f32[128,4,4,128]{0,3,2,1:T(8,128)} fusion(f32[4,1024,128,4]{2,1,3,0:T(8,128)} %get-tuple-element.280, pred[128,1024]{0,1:T(8,128)(4,1)S(1)} %and_and_fusion.2, bf16[1024,2,4,128]{3,0,2,1:T(8,128)(2,1)S(1)} %dynamic-slice_bitcast_fusion.2, f32[128,4,4,128]{0,3,2,1:T(8,128)} %get-tuple-element.295, pred[]{:T(512)S(6)} %compare.10), kind=kOutput, calls=%fused_computation.11.clone.1 | convolution fusion | flops 543686656 | bytes 11665409 | tf_op jit(solution)/shard_map/while/body/eval_jaxpr/tkgs,skd->tkgd/dot_general | solution.py:181
  222.4 0.9 and_and_fusion.2
  223.3 1.7 dynamic-slice_bitcast_fusion.2
  225.0 4.9 %fusion.56 = (f32[128,4,4]{0,2,1:T(4,128)S(1)}, f32[4,1024,128,4]{2,1,3,0:T(8,128)}) fusion(pred[128,1024]{0,1:T(8,128)(4,1)S(1)} %and_and_fusion.2, bf16[128,4,4,128]{3,0,2,1:T(8,128)(2,1)S(1)} %get-tuple-element.313, bf16[1024,2,4,128]{3,0,2,1:T(8,128)(2,1)S(1)} %dynamic-slice_bitcast_fusion.2), kind=kOutput, calls=%fused_computation.4.clone.1 | convolution fusion | flops 543160320 | bytes 10100736 | tf_op jit(solution)/shard_map/while/body/eval_jaxpr/tkgd,skd->tkgs/dot_general | solution.py:176
  230.0 6.0 %fusion.57 = f32[128,4,4,128]{0,3,2,1:T(8,128)} fusion(f32[4,1024,128,4]{2,1,3,0:T(8,128)} %get-tuple-element.280, pred[128,1024]{0,1:T(8,128)(4,1)S(1)} %and_and_fusion.2, bf16[1024,2,4,128]{3,0,2,1:T(8,128)(2,1)S(1)} %dynamic-slice_bitcast_fusion.2, f32[128,4,4,128]{0,3,2,1:T(8,128)} %get-tuple-element.295, pred[]{:T(512)S(6)} %compare.10), kind=kOutput, calls=%fused_computation.11.clone.1 | convolution fusion | flops 543686656 | bytes 11665409 | tf_op jit(solution)/shard_map/while/body/eval_jaxpr/tkgs,skd->tkgd/dot_general | solution.py:181
  236.0 1.3 divide_convert_fusion
  237.4 1.0 copy.105
  (131 shorter events, 13.1 us)
Async XLA Ops:
  6.5 116.8 %all-gather.3.cloned.1.call-start = ((), (), s32[]{:S(2)}) async-start(), calls=%async_computation | async-start | bytes 2088960 | tf_op jit(solution)/shard_map/all_gather | solution.py:104
  6.5 59.8 %collective-permute-start = (bf16[1,16,2048]{2,1,0:T(8,128)(2,1)}, bf16[1,16,2048]{2,1,0:T(8,128)(2,1)S(1)}, u32[]{:S(2)}, u32[]{:S(2)}) collective-permute-start(bf16[1,16,2048]{2,1,0:T(8,128)(2,1)} %param.21), channel_id=1, source_target_pairs={{0,2},{2,4},{4,6},{6,8},{8,10},{10,12},{12,14},{14,16},{16,18},{18... | collective-permute-start | bytes 196616 | tf_op jit(solution)/shard_map/ppermute | solution.py:26
  9.5 65.5 %collective-permute-start.8 = (bf16[1,16,2048]{2,1,0:T(8,128)(2,1)}, bf16[1,16,2048]{2,1,0:T(8,128)(2,1)S(1)}, u32[]{:S(2)}, u32[]{:S(2)}) collective-permute-start(bf16[1,16,2048]{2,1,0:T(8,128)(2,1)} %param.21), channel_id=1, source_target_pairs={{2,0},{4,2},{6,4},{8,6},{10,8},{12,10},{14,12},{16,14},{18,16},{20... | collective-permute-start | bytes 196616 | tf_op jit(solution)/shard_map/ppermute | solution.py:28
  13.5 191.5 %all-gather.5.cloned.1.call-start = ((), (), s32[]{:S(2)}) async-start(), calls=%async_computation.1 | async-start | bytes 4456448 | tf_op jit(solution)/shard_map/all_gather | solution.py:158
  20.0 103.3 %copy-start.18 = (s32[2]{0:T(128)}, s32[2]{0:T(128)S(1)}, u32[]{:S(2)}) copy-start(s32[2]{0:T(128)S(1)} %slice.44) | copy-start | bytes 28
  20.0 3.6 %copy-start.15 = (bf16[1,2,16,512]{3,2,1,0:T(8,128)(2,1)S(1)}, bf16[1,2,16,512]{3,2,1,0:T(8,128)(2,1)}, u32[]{:S(2)}) copy-start(bf16[1,2,16,512]{3,2,1,0:T(8,128)(2,1)} %param.22) | copy-start | bytes 98308
  20.0 71.3 %copy-start.16 = (s32[4]{0:T(128)S(1)}, s32[4]{0:T(128)}, u32[]{:S(2)}) copy-start(s32[4]{0:T(128)} %param.23) | copy-start | bytes 52
  20.0 72.1 %copy-start.21 = (bf16[128]{0:T(256)(128)(2,1)S(1)}, bf16[128]{0:T(256)(128)(2,1)}, u32[]{:S(2)}) copy-start(bf16[128]{0:T(256)(128)(2,1)} %param.19) | copy-start | bytes 772
  20.0 72.7 %copy-start.22 = (bf16[128]{0:T(256)(128)(2,1)S(1)}, bf16[128]{0:T(256)(128)(2,1)}, u32[]{:S(2)}) copy-start(bf16[128]{0:T(256)(128)(2,1)} %param.18) | copy-start | bytes 772
  66.4 25.6 %copy-start.2 = (bf16[1,16,2048]{2,1,0:T(8,128)(2,1)}, bf16[1,16,2048]{2,1,0:T(8,128)(2,1)S(1)}, u32[]{:S(2)}) copy-start(bf16[1,16,2048]{2,1,0:T(8,128)(2,1)S(1)} %collective-permute-done) | copy-start | bytes 196612
  66.4 8.6 %collective-permute-start.1 = (bf16[1,16,2048]{2,1,0:T(8,128)(2,1)S(1)}, bf16[1,16,2048]{2,1,0:T(8,128)(2,1)S(1)}, u32[]{:S(2)}, u32[]{:S(2)}) collective-permute-start(bf16[1,16,2048]{2,1,0:T(8,128)(2,1)S(1)} %collective-permute-done), channel_id=1, source_target_pairs={{0,2},{2,4},{4,6},{6,8},{8,10},{10,12},{12,14},{14,16},{16,18},{18... | collective-permute-start | bytes 196616 | tf_op jit(solution)/shard_map/ppermute | solution.py:26
  75.0 17.0 %copy-start.3 = (bf16[1,16,2048]{2,1,0:T(8,128)(2,1)}, bf16[1,16,2048]{2,1,0:T(8,128)(2,1)S(1)}, u32[]{:S(2)}) copy-start(bf16[1,16,2048]{2,1,0:T(8,128)(2,1)S(1)} %collective-permute-done.1) | copy-start | bytes 196612
  75.0 7.9 %collective-permute-start.2 = (bf16[1,16,2048]{2,1,0:T(8,128)(2,1)S(1)}, bf16[1,16,2048]{2,1,0:T(8,128)(2,1)S(1)}, u32[]{:S(2)}, u32[]{:S(2)}) collective-permute-start(bf16[1,16,2048]{2,1,0:T(8,128)(2,1)S(1)} %collective-permute-done.1), channel_id=1, source_target_pairs={{0,2},{2,4},{4,6},{6,8},{8,10},{10,12},{12,14},{14,16},{16,18},{18... | collective-permute-start | bytes 196616 | tf_op jit(solution)/shard_map/ppermute | solution.py:26
  75.0 17.0 %copy-start.1 = (bf16[1,16,2048]{2,1,0:T(8,128)(2,1)}, bf16[1,16,2048]{2,1,0:T(8,128)(2,1)S(1)}, u32[]{:S(2)}) copy-start(bf16[1,16,2048]{2,1,0:T(8,128)(2,1)S(1)} %collective-permute-done.8) | copy-start | bytes 196612
  75.0 7.9 %collective-permute-start.9 = (bf16[1,16,2048]{2,1,0:T(8,128)(2,1)S(1)}, bf16[1,16,2048]{2,1,0:T(8,128)(2,1)S(1)}, u32[]{:S(2)}, u32[]{:S(2)}) collective-permute-start(bf16[1,16,2048]{2,1,0:T(8,128)(2,1)S(1)} %collective-permute-done.8), channel_id=1, source_target_pairs={{2,0},{4,2},{6,4},{8,6},{10,8},{12,10},{14,12},{16,14},{18,16},{20... | collective-permute-start | bytes 196616 | tf_op jit(solution)/shard_map/ppermute | solution.py:28
  82.9 9.1 %copy-start.6 = (bf16[1,16,2048]{2,1,0:T(8,128)(2,1)}, bf16[1,16,2048]{2,1,0:T(8,128)(2,1)S(1)}, u32[]{:S(2)}) copy-start(bf16[1,16,2048]{2,1,0:T(8,128)(2,1)S(1)} %collective-permute-done.2) | copy-start | bytes 196612
  82.9 8.0 %collective-permute-start.3 = (bf16[1,16,2048]{2,1,0:T(8,128)(2,1)S(1)}, bf16[1,16,2048]{2,1,0:T(8,128)(2,1)S(1)}, u32[]{:S(2)}, u32[]{:S(2)}) collective-permute-start(bf16[1,16,2048]{2,1,0:T(8,128)(2,1)S(1)} %collective-permute-done.2), channel_id=1, source_target_pairs={{0,2},{2,4},{4,6},{6,8},{8,10},{10,12},{12,14},{14,16},{16,18},{18... | collective-permute-start | bytes 196616 | tf_op jit(solution)/shard_map/ppermute | solution.py:26
  82.9 42.9 %copy-start.4 = (bf16[1,16,2048]{2,1,0:T(8,128)(2,1)}, bf16[1,16,2048]{2,1,0:T(8,128)(2,1)S(1)}, u32[]{:S(2)}) copy-start(bf16[1,16,2048]{2,1,0:T(8,128)(2,1)S(1)} %collective-permute-done.9) | copy-start | bytes 196612
  83.0 10.3 %collective-permute-start.10 = (bf16[1,16,2048]{2,1,0:T(8,128)(2,1)S(1)}, bf16[1,16,2048]{2,1,0:T(8,128)(2,1)S(1)}, u32[]{:S(2)}, u32[]{:S(2)}) collective-permute-start(bf16[1,16,2048]{2,1,0:T(8,128)(2,1)S(1)} %collective-permute-done.9), channel_id=1, source_target_pairs={{2,0},{4,2},{6,4},{8,6},{10,8},{12,10},{14,12},{16,14},{18,16},{20... | collective-permute-start | bytes 196616 | tf_op jit(solution)/shard_map/ppermute | solution.py:28
  90.9 39.1 %copy-start.9 = (bf16[1,16,2048]{2,1,0:T(8,128)(2,1)}, bf16[1,16,2048]{2,1,0:T(8,128)(2,1)S(1)}, u32[]{:S(2)}) copy-start(bf16[1,16,2048]{2,1,0:T(8,128)(2,1)S(1)} %collective-permute-done.3) | copy-start | bytes 196612
  90.9 8.0 %collective-permute-start.4 = (bf16[1,16,2048]{2,1,0:T(8,128)(2,1)S(1)}, bf16[1,16,2048]{2,1,0:T(8,128)(2,1)S(1)}, u32[]{:S(2)}, u32[]{:S(2)}) collective-permute-start(bf16[1,16,2048]{2,1,0:T(8,128)(2,1)S(1)} %collective-permute-done.3), channel_id=1, source_target_pairs={{0,2},{2,4},{4,6},{6,8},{8,10},{10,12},{12,14},{14,16},{16,18},{18... | collective-permute-start | bytes 196616 | tf_op jit(solution)/shard_map/ppermute | solution.py:26
  93.2 36.8 %copy-start.7 = (bf16[1,16,2048]{2,1,0:T(8,128)(2,1)}, bf16[1,16,2048]{2,1,0:T(8,128)(2,1)S(1)}, u32[]{:S(2)}) copy-start(bf16[1,16,2048]{2,1,0:T(8,128)(2,1)S(1)} %collective-permute-done.10) | copy-start | bytes 196612
  93.2 8.0 %collective-permute-start.11 = (bf16[1,16,2048]{2,1,0:T(8,128)(2,1)S(1)}, bf16[1,16,2048]{2,1,0:T(8,128)(2,1)S(1)}, u32[]{:S(2)}, u32[]{:S(2)}) collective-permute-start(bf16[1,16,2048]{2,1,0:T(8,128)(2,1)S(1)} %collective-permute-done.10), channel_id=1, source_target_pairs={{2,0},{4,2},{6,4},{8,6},{10,8},{12,10},{14,12},{16,14},{18,16},{20... | collective-permute-start | bytes 196616 | tf_op jit(solution)/shard_map/ppermute | solution.py:28
  98.8 24.4 %copy-start.11 = (bf16[1,16,2048]{2,1,0:T(8,128)(2,1)}, bf16[1,16,2048]{2,1,0:T(8,128)(2,1)S(1)}, u32[]{:S(2)}) copy-start(bf16[1,16,2048]{2,1,0:T(8,128)(2,1)S(1)} %collective-permute-done.4) | copy-start | bytes 196612
  98.8 8.5 %collective-permute-start.5 = (bf16[1,16,2048]{2,1,0:T(8,128)(2,1)S(1)}, bf16[1,16,2048]{2,1,0:T(8,128)(2,1)S(1)}, u32[]{:S(2)}, u32[]{:S(2)}) collective-permute-start(bf16[1,16,2048]{2,1,0:T(8,128)(2,1)S(1)} %collective-permute-done.4), channel_id=1, source_target_pairs={{0,2},{2,4},{4,6},{6,8},{8,10},{10,12},{12,14},{14,16},{16,18},{18... | collective-permute-start | bytes 196616 | tf_op jit(solution)/shard_map/ppermute | solution.py:26
  101.2 22.0 %copy-start.12 = (bf16[1,16,2048]{2,1,0:T(8,128)(2,1)}, bf16[1,16,2048]{2,1,0:T(8,128)(2,1)S(1)}, u32[]{:S(2)}) copy-start(bf16[1,16,2048]{2,1,0:T(8,128)(2,1)S(1)} %collective-permute-done.11) | copy-start | bytes 196612
  101.2 8.0 %collective-permute-start.12 = (bf16[1,16,2048]{2,1,0:T(8,128)(2,1)S(1)}, bf16[1,16,2048]{2,1,0:T(8,128)(2,1)S(1)}, u32[]{:S(2)}, u32[]{:S(2)}) collective-permute-start(bf16[1,16,2048]{2,1,0:T(8,128)(2,1)S(1)} %collective-permute-done.11), channel_id=1, source_target_pairs={{2,0},{4,2},{6,4},{8,6},{10,8},{12,10},{14,12},{16,14},{18,16},{20... | collective-permute-start | bytes 196616 | tf_op jit(solution)/shard_map/ppermute | solution.py:28
  107.3 7.9 %collective-permute-start.6 = (bf16[1,16,2048]{2,1,0:T(8,128)(2,1)S(1)}, bf16[1,16,2048]{2,1,0:T(8,128)(2,1)S(1)}, u32[]{:S(2)}, u32[]{:S(2)}) collective-permute-start(bf16[1,16,2048]{2,1,0:T(8,128)(2,1)S(1)} %collective-permute-done.5), channel_id=1, source_target_pairs={{0,2},{2,4},{4,6},{6,8},{8,10},{10,12},{12,14},{14,16},{16,18},{18... | collective-permute-start | bytes 196616 | tf_op jit(solution)/shard_map/ppermute | solution.py:26
  109.2 14.0 %copy-start.14 = (bf16[1,16,2048]{2,1,0:T(8,128)(2,1)}, bf16[1,16,2048]{2,1,0:T(8,128)(2,1)S(1)}, u32[]{:S(2)}) copy-start(bf16[1,16,2048]{2,1,0:T(8,128)(2,1)S(1)} %collective-permute-done.12) | copy-start | bytes 196612
  109.2 7.9 %collective-permute-start.13 = (bf16[1,16,2048]{2,1,0:T(8,128)(2,1)S(1)}, bf16[1,16,2048]{2,1,0:T(8,128)(2,1)}, u32[]{:S(2)}, u32[]{:S(2)}) collective-permute-start(bf16[1,16,2048]{2,1,0:T(8,128)(2,1)S(1)} %collective-permute-done.12), channel_id=1, source_target_pairs={{2,0},{4,2},{6,4},{8,6},{10,8},{12,10},{14,12},{16,14},{18,16},{20... | collective-permute-start | bytes 196616 | tf_op jit(solution)/shard_map/ppermute | solution.py:28
  115.2 8.0 %collective-permute-start.7 = (bf16[1,16,2048]{2,1,0:T(8,128)(2,1)S(1)}, bf16[1,16,2048]{2,1,0:T(8,128)(2,1)S(1)}, u32[]{:S(2)}, u32[]{:S(2)}) collective-permute-start(bf16[1,16,2048]{2,1,0:T(8,128)(2,1)S(1)} %collective-permute-done.6), channel_id=1, source_target_pairs={{0,2},{2,4},{4,6},{6,8},{8,10},{10,12},{12,14},{14,16},{16,18},{18... | collective-permute-start | bytes 196616 | tf_op jit(solution)/shard_map/ppermute | solution.py:26
  117.1 21.1 %collective-permute-start.14 = (bf16[1,16,2048]{2,1,0:T(8,128)(2,1)}, bf16[1,16,2048]{2,1,0:T(8,128)(2,1)}, u32[]{:S(2)}, u32[]{:S(2)}) collective-permute-start(bf16[1,16,2048]{2,1,0:T(8,128)(2,1)} %collective-permute-done.13), channel_id=1, source_target_pairs={{2,0},{4,2},{6,4},{8,6},{10,8},{12,10},{14,12},{16,14},{18,16},{20... | collective-permute-start | bytes 196616 | tf_op jit(solution)/shard_map/ppermute | solution.py:28
  125.6 10.0 %copy-start = (bf16[1,16,2048]{2,1,0:T(8,128)(2,1)S(1)}, bf16[1,16,2048]{2,1,0:T(8,128)(2,1)}, u32[]{:S(2)}) copy-start(bf16[1,16,2048]{2,1,0:T(8,128)(2,1)} %param.21) | copy-start | bytes 196612
  125.8 10.7 %copy-start.13 = (bf16[1,16,2048]{2,1,0:T(8,128)(2,1)S(1)}, bf16[1,16,2048]{2,1,0:T(8,128)(2,1)}, u32[]{:S(2)}) copy-start(bf16[1,16,2048]{2,1,0:T(8,128)(2,1)} %copy-done.12) | copy-start | bytes 196612
  129.7 6.8 %copy-start.5 = (bf16[1,16,2048]{2,1,0:T(8,128)(2,1)S(1)}, bf16[1,16,2048]{2,1,0:T(8,128)(2,1)}, u32[]{:S(2)}) copy-start(bf16[1,16,2048]{2,1,0:T(8,128)(2,1)} %copy-done.4) | copy-start | bytes 196612
  130.0 3.1 %copy-start.10 = (bf16[1,16,2048]{2,1,0:T(8,128)(2,1)S(1)}, bf16[1,16,2048]{2,1,0:T(8,128)(2,1)}, u32[]{:S(2)}) copy-start(bf16[1,16,2048]{2,1,0:T(8,128)(2,1)} %copy-done.9) | copy-start | bytes 196612
  130.0 6.5 %copy-start.8 = (bf16[1,16,2048]{2,1,0:T(8,128)(2,1)S(1)}, bf16[1,16,2048]{2,1,0:T(8,128)(2,1)}, u32[]{:S(2)}) copy-start(bf16[1,16,2048]{2,1,0:T(8,128)(2,1)} %copy-done.7) | copy-start | bytes 196612
  130.1 9.7 %copy-start.19 = (s32[2]{0:T(128)S(1)}, s32[2]{0:T(128)}, u32[]{:S(2)}) copy-start(s32[2]{0:T(128)} %copy-done.18) | copy-start | bytes 28
  141.4 6.3 %copy-start.20 = (f32[128]{0:T(128)S(1)}, f32[128]{0:T(128)}, u32[]{:S(2)}) copy-start(f32[128]{0:T(128)} %convert_element_type.76) | copy-start | bytes 1540
  147.7 57.3 %copy-start.17 = (s32[1,4]{1,0:T(1,128)S(1)}, s32[1,4]{1,0:T(1,128)}, u32[]{:S(2)}) copy-start(s32[1,4]{1,0:T(1,128)} %broadcast_in_dim.65) | copy-start | bytes 52
  147.7 57.3 %copy-start.23 = (s32[2]{0:T(128)S(1)}, s32[2]{0:T(128)}, u32[]{:S(2)}) copy-start(s32[2]{0:T(128)} %iota_multiply_fusion) | copy-start | bytes 28
Sparse Core Ops, SparseCore 0:
  13.6 64.5 all-gather.2
  132.4 72.5 all-gather.4
